TPU v7x, 256 devices: a whole 4x4x8 slice. The times are simulated.
256 devices in a mesh: dp: 16 (over z, core), mp: 16 (over y, x).
Axes of the slice: x: 4, y: 4, z: 8, core: 2. Of those that a mesh axis runs over, the one named last changes fastest.
Arguments:
- intermediate_signal: bfloat16 [16, 1024, 14336], P('mp', None, 'dp'), may hold values from -6 to 6
- frozen_down_weight: bfloat16 [14336, 4096], P('dp', 'mp'), may hold values from -0.046875 to 0.046875
- lowdim_entry_matrices: bfloat16 [16, 16, 14336, 64], P('mp', None, 'dp'), may hold values from -0.046875 to 0.046875
- lowdim_exit_matrices: bfloat16 [16, 16, 64, 4096], P('mp', 'dp'), may hold values from -0.75 to 0.75
- result_sensitivity: bfloat16 [16, 1024, 4096], P('mp', 'dp'), may hold values from -6 to 6
- token_client_choice: int32 [16, 1024], P('mp'), may hold values from 0 to 15, as said below
- matrix_bank_position: int32 [16, 16], P('mp'), may hold values from 0 to 15, as said below
- shard_active_entries: int32 [16, 16], P('mp'), may hold values from 32 to 64, as said below
Outputs:
- customized_projection_result: bfloat16 [16, 1024, 4096], P('mp', 'dp')
- entry_matrix_derivative: float32 [16, 16, 14336, 64], P('mp', None, 'dp')
- exit_matrix_derivative: float32 [16, 16, 64, 4096], P('mp', 'dp')
Inputs may be any that keep to these rules, and one draw needn't show every extreme that they name: `token_client_choice`: rows s * 64 to (s + 1) * 64 - 1 of a group belong to device s of dp. The owner of adapter u is matrix_bank_position[u]. Of one device's live rows at most 8 have adapters of one owner, and in every group one owner gets exactly 8 live rows from every device. `matrix_bank_position`: in each group a permutation of the slots. The live rows of a device are its first shard_active_entries rows; in each group some device has 64.
All inputs are finite; a program needn't handle non-finite values.
Results may differ from a plain program's by a relative error of at most 0.0065.
Values may be sent and summed in bfloat16 or wider, within the bound.
A program may use at most 128 MiB of HBM per device.

v0:
```python
import jax
import jax.numpy as jnp
from jax import lax
from jax.sharding import PartitionSpec as P


def route_tables(user_ids, slot_table, counts, tok_dev, capacity, adapters_per_device):
    dp_size = counts.shape[0]
    row_total = user_ids.shape[0]
    adapter_list = slot_table.shape[0]
    adapter_range = jnp.arange(adapter_list, dtype=jnp.int32)
    named = user_ids[:, None] == adapter_range[None, :]
    storage = jnp.sum(jnp.where(named, slot_table[None, :], 0), axis=1)
    row_ids = jnp.arange(row_total, dtype=jnp.int32)
    source_of = row_ids // tok_dev
    by_source = source_of[:, None] == jnp.arange(dp_size, dtype=jnp.int32)[None, :]
    row_limit = jnp.sum(jnp.where(by_source, counts[None, :], 0), axis=1)
    is_live = row_ids % tok_dev < row_limit
    owners = storage // adapters_per_device
    local_slot = storage % adapters_per_device
    owner_marks = (
        (owners[:, None] == jnp.arange(dp_size, dtype=jnp.int32)[None, :]) & is_live[:, None]
    ).astype(jnp.int32)
    per_source = owner_marks.reshape(dp_size, tok_dev, dp_size)
    earlier = jnp.cumsum(per_source, axis=1) - per_source
    row_rank = jnp.sum(earlier * per_source, axis=2)
    slot_hits = per_source[:, :, :, None] * (
        row_rank[:, :, None, None] == jnp.arange(capacity, dtype=jnp.int32)[None, None, None, :]
    ).astype(jnp.int32)
    filled = jnp.sum(slot_hits, axis=1)
    slot_row = (
        jnp.sum(slot_hits * jnp.arange(tok_dev, dtype=jnp.int32)[None, :, None, None], axis=1)
        + (1 - filled) * tok_dev
    )
    slot_adapter = jnp.sum(
        slot_hits * local_slot.reshape(dp_size, tok_dev)[:, :, None, None], axis=1
    )
    choose = ((storage[:, None] == adapter_range[None, :]) & is_live[:, None]).astype(jnp.float32)
    return (choose, slot_row, filled, slot_adapter)


def split_parts(values):
    upper = values.astype(jnp.bfloat16)
    lower = (values - upper.astype(jnp.float32)).astype(jnp.bfloat16)
    return (upper, lower)


def on_device(
    intermediate_signal,
    frozen_down_weight,
    lowdim_entry_matrices,
    lowdim_exit_matrices,
    result_sensitivity,
    token_client_choice,
    matrix_bank_position,
    shard_active_entries,
):
    my_index = lax.axis_index("dp")
    dp_size = lax.axis_size("dp")
    device_rows = intermediate_signal[0]
    row_total = device_rows.shape[0]
    tok_dev = row_total // dp_size
    capacity = tok_dev // 8
    adapters_per_device = lowdim_exit_matrices.shape[1]
    adapter_rank_width = lowdim_exit_matrices.shape[2]
    feature_count = lowdim_exit_matrices.shape[3]
    choose, slot_row, filled, slot_adapter = route_tables(
        token_client_choice[0],
        matrix_bank_position[0],
        shard_active_entries[0],
        tok_dev,
        capacity,
        adapters_per_device,
    )
    base_part = jnp.dot(
        device_rows,
        lax.all_gather(frozen_down_weight, "mp", axis=1, tiled=True),
        preferred_element_type=jnp.float32,
    )
    rank_everything = jnp.einsum(
        "xz,szu->xsu", device_rows, lowdim_entry_matrices[0], preferred_element_type=jnp.float32
    )
    rank_part = jnp.sum(rank_everything * choose[:, :, None], axis=1)
    base_own, rank_own = (
        lax.psum_scatter(base_part, "dp", scatter_dimension=0, tiled=True),
        lax.psum_scatter(rank_part, "dp", scatter_dimension=0, tiled=True),
    )
    my_slots = lax.dynamic_index_in_dim(slot_row, my_index, 0, keepdims=False)
    padded_rank = jnp.concatenate(
        [rank_own, jnp.zeros((1, adapter_rank_width), jnp.float32)], axis=0
    )
    padded_grad = jnp.concatenate(
        [result_sensitivity[0], jnp.zeros((1, feature_count), jnp.bfloat16)], axis=0
    )
    send_rank = padded_rank[my_slots]
    send_grad = padded_grad[my_slots].astype(jnp.float32)
    recv_rank, recv_grad = (
        lax.all_to_all(send_rank, "dp", split_axis=0, concat_axis=0, tiled=True),
        lax.all_to_all(send_grad, "dp", split_axis=0, concat_axis=0, tiled=True),
    )
    flat_rank = recv_rank.reshape(dp_size * capacity, adapter_rank_width)
    flat_grad = recv_grad.reshape(dp_size * capacity, feature_count).astype(jnp.bfloat16)
    mine_adapter = lax.dynamic_index_in_dim(slot_adapter, my_index, 1, keepdims=False).reshape(-1)
    mine_filled = lax.dynamic_index_in_dim(filled, my_index, 1, keepdims=False)
    marks = ((mine_adapter == 0) & (mine_filled.reshape(-1) > 0))[:, None]
    rank_upper, rank_lower = split_parts(flat_rank * marks.astype(jnp.float32))
    masked_grad = flat_grad * marks.astype(jnp.bfloat16)
    output_map_weight = lowdim_exit_matrices[0, 0]
    adapter_contribution = jnp.dot(
        rank_upper, output_map_weight, preferred_element_type=jnp.float32
    ) + jnp.dot(rank_lower, output_map_weight, preferred_element_type=jnp.float32)
    outer_dims = (((0,), (0,)), ((), ()))
    derivative_fragments = [
        lax.dot_general(rank_upper, flat_grad, outer_dims, preferred_element_type=jnp.float32)
        + lax.dot_general(rank_lower, flat_grad, outer_dims, preferred_element_type=jnp.float32)
    ]
    rank_back = lax.dot_general(
        masked_grad, output_map_weight, (((1,), (1,)), ((), ())), preferred_element_type=jnp.float32
    )
    exit_matrix_derivative = jnp.stack(derivative_fragments)[None]
    rank_grad = rank_back.reshape(dp_size, capacity, adapter_rank_width)
    returned = lax.all_to_all(
        adapter_contribution.reshape(dp_size, capacity, feature_count),
        "dp",
        split_axis=0,
        concat_axis=0,
        tiled=True,
    )
    placed = (
        jnp.zeros((tok_dev + 1, feature_count), jnp.float32)
        .at[my_slots.reshape(-1)]
        .add(returned.reshape(-1, feature_count))
    )
    total = base_own + placed[:tok_dev]
    customized_projection_result = total.astype(jnp.bfloat16)
    gathered = lax.all_gather(rank_grad[None], "dp", axis=0, tiled=True)
    owner_view = jnp.transpose(slot_row, (1, 0, 2))
    owner_filled = jnp.transpose(filled, (1, 0, 2))
    spots = jnp.where(
        owner_filled > 0,
        jnp.arange(dp_size, dtype=jnp.int32)[None, :, None] * tok_dev + owner_view,
        row_total,
    ).reshape(-1)
    rank_grad_rows = (
        jnp.zeros((row_total, adapter_rank_width), jnp.float32)
        .at[spots]
        .add(gathered.reshape(-1, adapter_rank_width), mode="drop")
    )
    grad_upper, grad_lower = split_parts(rank_grad_rows)
    choose_marks = choose.astype(jnp.bfloat16)[:, :, None]
    entry_matrix_derivative = jnp.einsum(
        "vg,vqh->qgh",
        device_rows,
        choose_marks * grad_upper[:, None, :],
        preferred_element_type=jnp.float32,
    )
    entry_matrix_derivative = entry_matrix_derivative + jnp.einsum(
        "vg,vqh->qgh",
        device_rows,
        choose_marks * grad_lower[:, None, :],
        preferred_element_type=jnp.float32,
    )
    return (
        customized_projection_result[None],
        entry_matrix_derivative[None],
        exit_matrix_derivative,
    )


def solution(mesh):
    in_specs = (
        P("mp", None, "dp"),
        P("dp", "mp"),
        P("mp", None, "dp", None),
        P("mp", "dp", None, None),
        P("mp", "dp", None),
        P("mp", None),
        P("mp", None),
        P("mp", None),
    )
    out_specs = (P("mp", "dp", None), P("mp", None, "dp", None), P("mp", "dp", None, None))
    return jax.shard_map(
        on_device, mesh=mesh, in_specs=in_specs, out_specs=out_specs, check_vma=False
    )
```

profile of v0, /device:TPU:1, one launch (start us, length us, event | category | flops | bytes accessed | tf_op | source)
XLA Modules:
  0.0 291.7 jit_solution(618486240489323896)
XLA Ops:
  8.1 0.7 all-gather.3.cloned.1.call-update
  8.8 0.8 select_reduce_fusion.2
  9.6 0.7 select_reduce_fusion.1
  10.4 0.6 fusion.48
  11.0 3.9 %fusion.11 = f32[1024,1024]{0,1:S(1)} fusion(bf16[896,1024]{0,1:T(8,128)(2,1)} %bitcast.91, bf16[1,1024,896]{2,1,0:T(8,128)(2,1)S(1)} %copy-done), kind=kOutput, calls=%fused_computation.20 | convolution fusion | flops 1879048192 | bytes 7864320
  14.8 0.5 multiply_reduce_fusion
  15.4 1.0 copy.67
  16.4 0.2 reduce-scatter.3.cloned.1.call-start
  16.6 74.1 %all-gather.3.cloned.1.call-done = bf16[896,4096]{1,0:T(8,128)(2,1)} async-done(((bf16[896,256]{1,0:T(8,128)(2,1)}), bf16[896,4096]{1,0:T(8,128)(2,1)}) %all-gather.3.cloned.1.call-update) | async-done | bytes 7340048 | tf_op jit(solution)/shard_map/all_gather | solution.py:77
  90.8 14.3 %fusion.13 = f32[1024,4096]{1,0:T(8,128)} fusion(bf16[896,4096]{1,0:T(8,128)(2,1)} %all-gather.3.cloned.1.call-done, bf16[1,1024,896]{2,1,0:T(8,128)(2,1)S(1)} %copy-done), kind=kOutput, calls=%fused_computation.22 | convolution fusion | flops 7516192768 | bytes 25952256 | tf_op jit(solution)/shard_map/dot_general | solution.py:75
  105.2 0.1 copy.63
  105.3 0.1 copy.64
  105.4 1.7 select_reduce_fusion
  107.2 0.3 fusion.37
  107.5 0.2 copy.65
  107.8 8.7 %multiply_reduce_fusion.1 = (s32[16,16,8]{2,1,0:T(8,128)S(1)}, s32[16,16,8]{2,1,0:T(8,128)S(1)}) fusion(s32[16,64,8]{1,2,0:T(8,128)S(1)} %fusion.43, s32[16,64,16]{1,2,0:T(8,128)S(1)} %copy.65), kind=kLoop, calls=%fused_computation.24 | loop fusion | flops 520192 | bytes 114688 | tf_op jit(solution)/shard_map/reduce_sum | solution.py:30
  116.5 0.7 select_bitcast_fusion
  117.3 0.1 copy.69
  117.4 0.1 reshape.336
  117.5 0.8 concatenate.6
  118.3 0.6 gather_fusion
  118.9 0.7 reshape.381
  119.7 9.1 %all-to-all-start = ((f32[16,1,512]{2,1,0:T(1,128)}), f32[16,1,512]{2,1,0:T(1,128)S(1)}, u32[]{:S(2)}, u32[]{:S(2)}) async-start(f32[16,1,512]{2,1,0:T(1,128)} %reshape.381), calls=%async_computation.2 | async-start | bytes 65536 | tf_op jit(solution)/shard_map/all_to_all | solution.py:98
  128.8 2.2 gather_fusion.1
  130.9 5.4 %all-to-all-done = f32[16,1,512]{2,1,0:T(1,128)S(1)} async-done(((f32[16,1,512]{2,1,0:T(1,128)}), f32[16,1,512]{2,1,0:T(1,128)S(1)}, u32[]{:S(2)}, u32[]{:S(2)}) %all-to-all-start) | async-done | bytes 32800 | tf_op jit(solution)/shard_map/all_to_all | solution.py:98
  136.3 0.6 copy-done.4
  136.9 3.9 %all-to-all-start.2 = ((bf16[16,8,4096]{2,1,0:T(8,128)(2,1)}), bf16[16,8,4096]{2,1,0:T(8,128)(2,1)S(1)}, u32[]{:S(2)}, u32[]{:S(2)}) async-start(bf16[16,8,4096]{2,1,0:T(8,128)(2,1)} %bitcast.84), calls=%async_computation.4 | async-start | bytes 2097152 | tf_op jit(solution)/shard_map/all_to_all | solution.py:99
  141.0 0.6 broadcast.315
  141.6 1.5 reduce
  143.0 0.1 reshape.382
  143.1 0.5 fusion.33
  143.6 1.8 fusion
  145.4 28.3 %all-to-all-done.2 = bf16[16,8,4096]{2,1,0:T(8,128)(2,1)S(1)} async-done(((bf16[16,8,4096]{2,1,0:T(8,128)(2,1)}), bf16[16,8,4096]{2,1,0:T(8,128)(2,1)S(1)}, u32[]{:S(2)}, u32[]{:S(2)}) %all-to-all-start.2) | async-done | bytes 1048608 | tf_op jit(solution)/shard_map/all_to_all | solution.py:99
  173.6 4.5 %all-to-all-start.1 = ((f32[16,8,4096]{2,1,0:T(8,128)}), f32[16,8,4096]{2,1,0:T(8,128)}, u32[]{:S(2)}, u32[]{:S(2)}) async-start(f32[16,8,4096]{2,1,0:T(8,128)} %fusion), calls=%async_computation.3 | async-start | bytes 4194304 | tf_op jit(solution)/shard_map/all_to_all | solution.py:122
  178.1 0.1 reshape.327
  178.2 1.6 copy.72
  179.8 1.0 reshape.330
  180.8 0.1 copy.73
  180.9 0.5 fusion.25
  181.4 75.7 %all-gather = f32[256,8,64]{2,1,0:T(8,128)} all-gather(f32[16,8,64]{2,1,0:T(8,128)S(1)} %fusion.25), channel_id=2, replica_groups=mesh['dp'=16,'mp'=16] {'dp'}, dimensions={0}, use_global_device_ids=true | all-gather | bytes 557056 | tf_op jit(solution)/shard_map/all_gather | solution.py:136
  257.1 11.0 %scatter_custom_fusion.1 = f32[1024,64]{1,0:T(8,128)S(1)} fusion(s32[2048]{0:T(1024)S(1)} %bitcast.87, f32[256,8,64]{2,1,0:T(8,128)} %all-gather, f32[]{:T(128)} %constant.81.clone.1), kind=kCustom, calls=%fused_computation.30 | custom fusion | flops 131072 | bytes 786436 | tf_op jit(solution)/shard_map/scatter-add | solution.py:147
  268.1 0.9 copy.74
  269.0 0.4 convolution_bitcast_fusion.1
  269.4 1.4 fusion.2
  270.9 2.3 fusion.5
  273.2 4.2 %add_bitcast_fusion = f32[1,16,896,64]{2,3,1,0:T(8,128)} fusion(f32[16,64,896]{2,1,0:T(8,128)S(1)} %fusion.5, bf16[1,1024,896]{2,1,0:T(8,128)(2,1)S(1)} %copy-done, bf16[1024,64]{0,1:T(8,128)(2,1)S(1)} %get-tuple-element.6, bf16[1024,16]{0,1:T(8,128)(2,1)S(1)} %copy-done.5), kind=kOutput, calls=%fused_computation.11 | convolution fusion | flops 1881014272 | bytes 9338880 | tf_op jit(solution)/shard_map/vg,vqh->qgh/dot_general | solution.py:151
  277.4 4.7 %scatter_custom_fusion = f32[65,4096]{1,0:T(8,128)S(1)} fusion(s32[128]{0:T(128)S(1)} %fusion.61, f32[16,8,4096]{2,1,0:T(8,128)} %all-to-all-done.1, f32[]{:T(128)} %constant.81.clone.1), kind=kCustom, calls=%fused_computation.12 | custom fusion | flops 524288 | bytes 3162116 | tf_op jit(solution)/shard_map/scatter-add | solution.py:132
  282.2 2.1 fusion.30
  (39 shorter events, 0.8 us)
Async XLA Ops:
  8.0 3.0 %copy-start = (bf16[1,1024,896]{2,1,0:T(8,128)(2,1)S(1)}, bf16[1,1024,896]{2,1,0:T(8,128)(2,1)}, u32[]{:S(2)}) copy-start(bf16[1,1024,896]{2,1,0:T(8,128)(2,1)} %param.8) | copy-start | bytes 5505028
  8.0 82.7 %all-gather.3.cloned.1.call-start = ((), (), s32[]{:S(2)}) async-start(), calls=%async_computation.5 | async-start | bytes 7798784 | tf_op jit(solution)/shard_map/all_gather | solution.py:77
  8.7 108.8 %reduce-scatter.5.cloned.1.call-start = ((), (), s32[]{:S(2)}) async-start(), calls=%async_computation.7 | async-start | bytes 557056 | tf_op jit(solution)/shard_map/reduce_scatter | solution.py:86
  16.4 265.8 %reduce-scatter.3.cloned.1.call-start = ((), (), s32[]{:S(2)}) async-start(), calls=%async_computation.6 | async-start | bytes 17825792 | tf_op jit(solution)/shard_map/reduce_scatter | solution.py:85
  105.0 23.7 %copy-start.3 = (bf16[1,64,4096]{2,1,0:T(8,128)(2,1)S(1)}, bf16[1,64,4096]{2,1,0:T(8,128)(2,1)}, u32[]{:S(2)}) copy-start(bf16[1,64,4096]{2,1,0:T(8,128)(2,1)} %param.12) | copy-start | bytes 1572868
  119.7 16.7 %all-to-all-start = ((f32[16,1,512]{2,1,0:T(1,128)}), f32[16,1,512]{2,1,0:T(1,128)S(1)}, u32[]{:S(2)}, u32[]{:S(2)}) async-start(f32[16,1,512]{2,1,0:T(1,128)} %reshape.381), calls=%async_computation.2 | async-start | bytes 65536 | tf_op jit(solution)/shard_map/all_to_all | solution.py:98
  130.9 12.2 %copy-start.1 = (bf16[1,1,64,4096]{3,2,1,0:T(8,128)(2,1)S(1)}, bf16[1,1,64,4096]{3,2,1,0:T(8,128)(2,1)}, u32[]{:S(2)}) copy-start(bf16[1,1,64,4096]{3,2,1,0:T(8,128)(2,1)} %param.11) | copy-start | bytes 1572868
  136.3 0.6 copy-start.4
  136.9 36.7 %all-to-all-start.2 = ((bf16[16,8,4096]{2,1,0:T(8,128)(2,1)}), bf16[16,8,4096]{2,1,0:T(8,128)(2,1)S(1)}, u32[]{:S(2)}, u32[]{:S(2)}) async-start(bf16[16,8,4096]{2,1,0:T(8,128)(2,1)} %bitcast.84), calls=%async_computation.4 | async-start | bytes 2097152 | tf_op jit(solution)/shard_map/all_to_all | solution.py:99
  173.6 103.8 %all-to-all-start.1 = ((f32[16,8,4096]{2,1,0:T(8,128)}), f32[16,8,4096]{2,1,0:T(8,128)}, u32[]{:S(2)}, u32[]{:S(2)}) async-start(f32[16,8,4096]{2,1,0:T(8,128)} %fusion), calls=%async_computation.3 | async-start | bytes 4194304 | tf_op jit(solution)/shard_map/all_to_all | solution.py:122
  269.4 1.4 copy-start.2
  269.4 1.4 copy-start.5
Sparse Core Ops, SparseCore 0:
  11.2 79.4 all-gather.2
Sparse Core Ops, SparseCore 1:
  16.5 59.3 reduce-scatter.4
  105.1 172.6 reduce-scatter.2
where the time goes:
time: 292 us
  waiting for transfers between devices  109 us (37%)
  blocking collectives  75.7 us (26%)
  other arithmetic  33.5 us (11%)
  matrix products  29.2 us (10%)
  starting transfers between devices  17.7 us (6%)
  between operations  15.7 us (5%)
  local copies, waits for them, and re-layouts  11.3 us (4%)
    all_gather x1, blocking collectives, on_device(): gathered = lax.all_gather(rank_grad[None], 'dp', axis=0, tiled=True)  75.7 us
    all_gather x1, waiting for transfers between devices, on_device(): lax.all_gather(frozen_down_weight, 'mp', axis=1, tiled=True)  74.1 us
    all_to_all x1, waiting for transfers between devices, on_device(): lax.all_to_all(send_grad, 'dp', split_axis=0, concat_axis=0, tiled=True)  28.3 us
    dot_general x1, matrix products, on_device(): jnp.dot(device_rows, lax.all_gather(frozen_down_weight, 'mp', axis=1, til...  14.3 us
    scatter-add x1, other arithmetic, on_device(): rank_grad_rows = jnp.zeros((row_total, adapter_rank_width), jnp.float32)....  11 us
    all_to_all x1, starting transfers between devices, on_device(): lax.all_to_all(send_rank, 'dp', split_axis=0, concat_axis=0, tiled=True)  9.05 us
    reduce_sum x1, other arithmetic, route_tables(): filled = jnp.sum(slot_hits, axis=1)  8.7 us
  transfers between devices with their start and end apart: 6, of which 3 were waited for; matrix products, arithmetic and copies ran while one was open for 24% of the time, Pallas kernels for 0%

commit v1 on v0

--- a/solution.py
+++ b/solution.py
@@ -2,6 +2,11 @@
 import jax.numpy as jnp
 from jax import lax
 from jax.sharding import PartitionSpec as P
+
+
+def all_by_exchange(value, axis, d):
+    sent = jnp.stack([value] * lax.axis_size(axis))
+    return jnp.concatenate(lax.all_to_all(sent, axis, 0, 0), axis=d)
 
 
 def route_tables(user_ids, slot_table, counts, tok_dev, capacity, adapters_per_device):
@@ -74,7 +79,7 @@
     )
     base_part = jnp.dot(
         device_rows,
-        lax.all_gather(frozen_down_weight, "mp", axis=1, tiled=True),
+        all_by_exchange(frozen_down_weight, "mp", 1),
         preferred_element_type=jnp.float32,
     )
     rank_everything = jnp.einsum(

time: 292 us -> 331 us (1.13)
  waiting for transfers between devices: 109 us -> 135 us
  starting transfers between devices: 17.7 us -> 26.6 us
  local copies, waits for them, and re-layouts: 11.3 us -> 16.7 us
    all_to_all x0 -> x1, waiting for transfers between devices: none -> 101 us  [all_by_exchange(): return jnp.concatenate(lax.all_to_all(sent, axis, 0, 0), axis=d)]
    all_gather x1 -> x0, waiting for transfers between devices: 74.1 us -> none  [on_device(): lax.all_gather(frozen_down_weight, 'mp', axis=1, tiled=True)]
    all_to_all x0 -> x1, starting transfers between devices: none -> 7.75 us  [all_by_exchange(): return jnp.concatenate(lax.all_to_all(sent, axis, 0, 0), axis=d)]
    another operation x0 -> x1, local copies, waits for them, and re-layouts: none -> 3.98 us  [all_by_exchange(): sent = jnp.stack([value] * lax.axis_size(axis))]
  transfers between devices with their start and end apart: 6 -> 6, of which waited for: 3 -> 3; matrix products, arithmetic and copies ran while one was open for 24% -> 21% of each run, Pallas kernels for 0% -> 0%
where the time goes in v1:
time: 331 us; the launch traced here: 330 us
  waiting for transfers between devices  135 us (41%)
  blocking collectives  75.7 us (23%)
  other arithmetic  32.2 us (10%)
  matrix products  29.2 us (9%)
  starting transfers between devices  26.6 us (8%)
  local copies, waits for them, and re-layouts  16.7 us (5%)
  between operations  14.3 us (4%)
    all_to_all x1, waiting for transfers between devices, all_by_exchange(): return jnp.concatenate(lax.all_to_all(sent, axis, 0, 0), axis=d)  101 us
    all_gather x1, blocking collectives, on_device(): gathered = lax.all_gather(rank_grad[None], 'dp', axis=0, tiled=True)  75.7 us
    all_to_all x1, waiting for transfers between devices, on_device(): lax.all_to_all(send_grad, 'dp', split_axis=0, concat_axis=0, tiled=True)  28.3 us
    dot_general x1, matrix products, on_device(): jnp.dot(device_rows, all_by_exchange(frozen_down_weight, 'mp', 1), prefer...  14.3 us
    scatter-add x1, other arithmetic, on_device(): rank_grad_rows = jnp.zeros((row_total, adapter_rank_width), jnp.float32)....  11 us
    all_to_all x1, starting transfers between devices, on_device(): lax.all_to_all(send_rank, 'dp', split_axis=0, concat_axis=0, tiled=True)  10.2 us
    reduce_sum x1, other arithmetic, route_tables(): filled = jnp.sum(slot_hits, axis=1)  8.7 us
    all_to_all x1, starting transfers between devices, all_by_exchange(): return jnp.concatenate(lax.all_to_all(sent, axis, 0, 0), axis=d)  7.75 us
  transfers between devices with their start and end apart: 6, of which 3 were waited for; matrix products, arithmetic and copies ran while one was open for 21% of the time, Pallas kernels for 0%

profile of v1, /device:TPU:1, one launch (start us, length us, event | category | flops | bytes accessed | tf_op | source)
XLA Modules:
  0.0 329.9 jit_solution(4218074610942494179)
XLA Ops:
  7.2 1.4 copy.66
  8.6 4.0 %stack.2 = bf16[16,896,256]{1,2,0:T(8,128)(2,1)} broadcast(bf16[896,256]{0,1:T(8,128)(2,1)S(1)} %copy.66), dimensions={1,2} | broadcast | bytes 7798784 | tf_op jit(solution)/shard_map/stack | solution.py:8
  12.6 7.7 %all-to-all-start = ((bf16[16,896,256]{1,2,0:T(8,128)(2,1)}), bf16[16,896,256]{1,2,0:T(8,128)(2,1)}, u32[]{:S(2)}, u32[]{:S(2)}) async-start(bf16[16,896,256]{1,2,0:T(8,128)(2,1)} %stack.2), calls=%async_computation | async-start | bytes 14680064 | tf_op jit(solution)/shard_map/all_to_all | solution.py:9
  20.4 0.1 select_reduce_fusion.2
  20.5 0.1 select_reduce_fusion.1
  20.6 0.6 fusion.48
  21.2 3.9 %fusion.11 = f32[1024,1024]{0,1:S(1)} fusion(bf16[896,1024]{0,1:T(8,128)(2,1)} %bitcast.94, bf16[1,1024,896]{2,1,0:T(8,128)(2,1)S(1)} %copy-done), kind=kOutput, calls=%fused_computation.20 | convolution fusion | flops 1879048192 | bytes 7864320
  25.1 0.5 multiply_reduce_fusion
  25.6 1.0 copy.71
  26.6 0.2 reduce-scatter.3.cloned.1.call-start
  26.9 101.5 %all-to-all-done = bf16[16,896,256]{1,2,0:T(8,128)(2,1)} async-done(((bf16[16,896,256]{1,2,0:T(8,128)(2,1)}), bf16[16,896,256]{1,2,0:T(8,128)(2,1)}, u32[]{:S(2)}, u32[]{:S(2)}) %all-to-all-start) | async-done | bytes 7340064 | tf_op jit(solution)/shard_map/all_to_all | solution.py:9
  128.3 14.3 %fusion.13 = f32[1024,4096]{1,0:T(8,128)} fusion(bf16[896,4096]{0,1:T(8,128)(2,1)} %bitcast.2, bf16[1,1024,896]{2,1,0:T(8,128)(2,1)S(1)} %copy-done), kind=kOutput, calls=%fused_computation.22 | convolution fusion | flops 7516192768 | bytes 25952256 | tf_op jit(solution)/shard_map/dot_general | solution.py:80
  142.8 0.1 copy.67
  142.9 0.1 copy.68
  143.0 1.7 select_reduce_fusion
  144.8 0.3 fusion.37
  145.1 0.2 copy.69
  145.4 8.7 %multiply_reduce_fusion.1 = (s32[16,16,8]{2,1,0:T(8,128)S(1)}, s32[16,16,8]{2,1,0:T(8,128)S(1)}) fusion(s32[16,64,8]{1,2,0:T(8,128)S(1)} %fusion.43, s32[16,64,16]{1,2,0:T(8,128)S(1)} %copy.69), kind=kLoop, calls=%fused_computation.24 | loop fusion | flops 520192 | bytes 114688 | tf_op jit(solution)/shard_map/reduce_sum | solution.py:35
  154.1 0.7 select_bitcast_fusion
  155.0 0.1 reshape.346
  155.1 0.8 concatenate.6
  155.9 0.6 gather_fusion
  156.5 0.7 reshape.391
  157.3 10.2 %all-to-all-start.1 = ((f32[16,1,512]{2,1,0:T(1,128)}), f32[16,1,512]{2,1,0:T(1,128)S(1)}, u32[]{:S(2)}, u32[]{:S(2)}) async-start(f32[16,1,512]{2,1,0:T(1,128)} %reshape.391), calls=%async_computation.3 | async-start | bytes 65536 | tf_op jit(solution)/shard_map/all_to_all | solution.py:103
  167.6 2.2 gather_fusion.1
  169.7 5.4 %all-to-all-done.1 = f32[16,1,512]{2,1,0:T(1,128)S(1)} async-done(((f32[16,1,512]{2,1,0:T(1,128)}), f32[16,1,512]{2,1,0:T(1,128)S(1)}, u32[]{:S(2)}, u32[]{:S(2)}) %all-to-all-start.1) | async-done | bytes 32800 | tf_op jit(solution)/shard_map/all_to_all | solution.py:103
  175.1 0.6 copy-done.4
  175.7 3.9 %all-to-all-start.3 = ((bf16[16,8,4096]{2,1,0:T(8,128)(2,1)}), bf16[16,8,4096]{2,1,0:T(8,128)(2,1)S(1)}, u32[]{:S(2)}, u32[]{:S(2)}) async-start(bf16[16,8,4096]{2,1,0:T(8,128)(2,1)} %bitcast.87), calls=%async_computation.5 | async-start | bytes 2097152 | tf_op jit(solution)/shard_map/all_to_all | solution.py:104
  179.7 0.6 broadcast.317
  180.3 1.5 reduce
  181.9 0.5 fusion.33
  182.3 1.8 fusion
  184.1 28.3 %all-to-all-done.3 = bf16[16,8,4096]{2,1,0:T(8,128)(2,1)S(1)} async-done(((bf16[16,8,4096]{2,1,0:T(8,128)(2,1)}), bf16[16,8,4096]{2,1,0:T(8,128)(2,1)S(1)}, u32[]{:S(2)}, u32[]{:S(2)}) %all-to-all-start.3) | async-done | bytes 1048608 | tf_op jit(solution)/shard_map/all_to_all | solution.py:104
  212.4 4.5 %all-to-all-start.2 = ((f32[16,8,4096]{2,1,0:T(8,128)}), f32[16,8,4096]{2,1,0:T(8,128)}, u32[]{:S(2)}, u32[]{:S(2)}) async-start(f32[16,8,4096]{2,1,0:T(8,128)} %fusion), calls=%async_computation.4 | async-start | bytes 4194304 | tf_op jit(solution)/shard_map/all_to_all | solution.py:127
  216.9 0.1 reshape.337
  217.0 1.6 copy.76
  218.6 1.0 reshape.340
  219.6 0.1 copy.77
  219.7 0.5 fusion.25
  220.2 75.7 %all-gather = f32[256,8,64]{2,1,0:T(8,128)} all-gather(f32[16,8,64]{2,1,0:T(8,128)S(1)} %fusion.25), channel_id=2, replica_groups=mesh['dp'=16,'mp'=16] {'dp'}, dimensions={0}, use_global_device_ids=true | all-gather | bytes 557056 | tf_op jit(solution)/shard_map/all_gather | solution.py:141
  295.9 11.0 %scatter_custom_fusion.1 = f32[1024,64]{1,0:T(8,128)S(1)} fusion(s32[2048]{0:T(1024)S(1)} %bitcast.90, f32[256,8,64]{2,1,0:T(8,128)} %all-gather, f32[]{:T(128)} %constant.81.clone.1), kind=kCustom, calls=%fused_computation.30 | custom fusion | flops 131072 | bytes 786436 | tf_op jit(solution)/shard_map/scatter-add | solution.py:152
  306.9 0.9 copy.78
  307.8 0.4 convolution_bitcast_fusion.1
  308.2 1.4 fusion.2
  309.6 2.3 fusion.5
  312.0 4.2 %add_bitcast_fusion = f32[1,16,896,64]{2,3,1,0:T(8,128)} fusion(f32[16,64,896]{2,1,0:T(8,128)S(1)} %fusion.5, bf16[1,1024,896]{2,1,0:T(8,128)(2,1)S(1)} %copy-done, bf16[1024,64]{0,1:T(8,128)(2,1)S(1)} %get-tuple-element.6, bf16[1024,16]{0,1:T(8,128)(2,1)S(1)} %copy-done.5), kind=kOutput, calls=%fused_computation.11 | convolution fusion | flops 1881014272 | bytes 9338880 | tf_op jit(solution)/shard_map/vg,vqh->qgh/dot_general | solution.py:156
  316.2 4.8 %scatter_custom_fusion = f32[65,4096]{1,0:T(8,128)S(1)} fusion(s32[128]{0:T(128)S(1)} %fusion.61, f32[16,8,4096]{2,1,0:T(8,128)} %all-to-all-done.2, f32[]{:T(128)} %constant.81.clone.1), kind=kCustom, calls=%fused_computation.12 | custom fusion | flops 524288 | bytes 3162116 | tf_op jit(solution)/shard_map/scatter-add | solution.py:137
  321.0 2.1 fusion.30
  (46 shorter events, 0.9 us)
Async XLA Ops:
  7.2 14.1 %copy-start = (bf16[1,1024,896]{2,1,0:T(8,128)(2,1)S(1)}, bf16[1,1024,896]{2,1,0:T(8,128)(2,1)}, u32[]{:S(2)}) copy-start(bf16[1,1024,896]{2,1,0:T(8,128)(2,1)} %param.8) | copy-start | bytes 5505028
  12.6 7.8 %copy-start.6 = (s32[1,1024]{1,0:T(1,128)S(1)}, s32[1,1024]{1,0:T(1,128)}, u32[]{:S(2)}) copy-start(s32[1,1024]{1,0:T(1,128)} %param.13) | copy-start | bytes 12292
  12.6 7.8 %copy-start.7 = (s32[1,16]{1,0:T(1,128)S(1)}, s32[1,16]{1,0:T(1,128)}, u32[]{:S(2)}) copy-start(s32[1,16]{1,0:T(1,128)} %param.14) | copy-start | bytes 196
  12.6 7.9 %copy-start.8 = (s32[1,16]{1,0:T(1,128)S(1)}, s32[1,16]{1,0:T(1,128)}, u32[]{:S(2)}) copy-start(s32[1,16]{1,0:T(1,128)} %param.15) | copy-start | bytes 196
  12.6 115.7 %all-to-all-start = ((bf16[16,896,256]{1,2,0:T(8,128)(2,1)}), bf16[16,896,256]{1,2,0:T(8,128)(2,1)}, u32[]{:S(2)}, u32[]{:S(2)}) async-start(bf16[16,896,256]{1,2,0:T(8,128)(2,1)} %stack.2), calls=%async_computation | async-start | bytes 14680064 | tf_op jit(solution)/shard_map/all_to_all | solution.py:9
  20.3 134.8 %reduce-scatter.5.cloned.1.call-start = ((), (), s32[]{:S(2)}) async-start(), calls=%async_computation.7 | async-start | bytes 557056 | tf_op jit(solution)/shard_map/reduce_scatter | solution.py:91
  26.6 294.4 %reduce-scatter.3.cloned.1.call-start = ((), (), s32[]{:S(2)}) async-start(), calls=%async_computation.6 | async-start | bytes 17825792 | tf_op jit(solution)/shard_map/reduce_scatter | solution.py:90
  142.7 24.9 %copy-start.3 = (bf16[1,64,4096]{2,1,0:T(8,128)(2,1)S(1)}, bf16[1,64,4096]{2,1,0:T(8,128)(2,1)}, u32[]{:S(2)}) copy-start(bf16[1,64,4096]{2,1,0:T(8,128)(2,1)} %param.12) | copy-start | bytes 1572868
  157.3 17.8 %all-to-all-start.1 = ((f32[16,1,512]{2,1,0:T(1,128)}), f32[16,1,512]{2,1,0:T(1,128)S(1)}, u32[]{:S(2)}, u32[]{:S(2)}) async-start(f32[16,1,512]{2,1,0:T(1,128)} %reshape.391), calls=%async_computation.3 | async-start | bytes 65536 | tf_op jit(solution)/shard_map/all_to_all | solution.py:103
  169.7 12.1 %copy-start.1 = (bf16[1,1,64,4096]{3,2,1,0:T(8,128)(2,1)S(1)}, bf16[1,1,64,4096]{3,2,1,0:T(8,128)(2,1)}, u32[]{:S(2)}) copy-start(bf16[1,1,64,4096]{3,2,1,0:T(8,128)(2,1)} %param.11) | copy-start | bytes 1572868
  175.1 0.6 copy-start.4
  175.7 36.7 %all-to-all-start.3 = ((bf16[16,8,4096]{2,1,0:T(8,128)(2,1)}), bf16[16,8,4096]{2,1,0:T(8,128)(2,1)S(1)}, u32[]{:S(2)}, u32[]{:S(2)}) async-start(bf16[16,8,4096]{2,1,0:T(8,128)(2,1)} %bitcast.87), calls=%async_computation.5 | async-start | bytes 2097152 | tf_op jit(solution)/shard_map/all_to_all | solution.py:104
  212.4 103.8 %all-to-all-start.2 = ((f32[16,8,4096]{2,1,0:T(8,128)}), f32[16,8,4096]{2,1,0:T(8,128)}, u32[]{:S(2)}, u32[]{:S(2)}) async-start(f32[16,8,4096]{2,1,0:T(8,128)} %fusion), calls=%async_computation.4 | async-start | bytes 4194304 | tf_op jit(solution)/shard_map/all_to_all | solution.py:127
  308.2 1.4 copy-start.2
  308.2 1.4 copy-start.5
Sparse Core Ops, SparseCore 0:
  26.7 59.9 reduce-scatter.4
  142.8 174.3 reduce-scatter.2
